TPU v7x, 128 devices: a whole 4x4x4 slice. The times are simulated.
128 devices in a mesh: expert: 16 (over x, y), head: 8 (over z, core).
Axes of the slice: x: 4, y: 4, z: 4, core: 2. Of those that a mesh axis runs over, the one named last changes fastest.
Arguments:
- table_cells: bfloat16 [8192, 2, 2048], P(('expert', 'head')), may hold values from -8 to 8
- w_query: bfloat16 [2048, 2048], P(None, 'head')
- w_key: bfloat16 [2048, 2048], P(None, 'head')
- w_value: bfloat16 [2048, 2048], P(None, 'head'), may hold values from -0.125 to 0.125
- w_out: bfloat16 [2048, 2048], P('head'), may hold values from -0.125 to 0.125
- norm_gain: bfloat16 [2048], replicated, may hold values from 0.099609375 to 1.8984375
- w_gate: bfloat16 [128, 704, 2048], P(('expert', 'head')), may hold values from -0.125 to 0.125
- w_up: bfloat16 [128, 704, 2048], P(('expert', 'head')), may hold values from -0.125 to 0.125
- w_down: bfloat16 [128, 704, 2048], P(('expert', 'head')), may hold values from -0.15625 to 0.15625
- lengths: int32 [2], replicated, may hold values from 2048 to 8192, as said below
- expert_of_cell: int32 [8192, 2], P(('expert', 'head')), may hold values from 0 to 63, as said below
- slot_of_cell: int32 [8192, 2], P(('expert', 'head')), may hold values from 0 to 3, as said below
Outputs:
- updated_cells: bfloat16 [8192, 2, 2048], P(('expert', 'head'))
Inputs may be any that keep to these rules, and one draw needn't show every extreme that they name: `lengths`: one table in every draw has all 8192 cells. `expert_of_cell`: within the 128 cells of one device (aligned blocks in row-major order), no expert has more than 4 cells, and in every draw one expert has exactly 4 cells in every device's block. `slot_of_cell`: cells of one device with the same expert have distinct slots.
All inputs are finite; a program needn't handle non-finite values.
Results may differ from a plain program's by a relative error of at most 0.014.
Values may be sent and summed in bfloat16 or wider, within the bound.
A program may use at most 128 MiB of HBM per device.

v0:
```python
import math
import jax
import jax.numpy as jnp
from jax import lax
from jax.sharding import PartitionSpec as P

DH = 128


def expert_half(slot_rows, gate_half, up_half, down_half):
    contract_rows = (((1,), (1,)), ((), ()))
    gate_t = lax.dot_general(
        gate_half, slot_rows, contract_rows, preferred_element_type=jnp.float32
    )
    up_t = lax.dot_general(up_half, slot_rows, contract_rows, preferred_element_type=jnp.float32)
    hidden = (jax.nn.silu(gate_t) * up_t).astype(jnp.bfloat16)
    product = lax.dot_general(
        hidden, down_half, (((0,), (0,)), ((), ())), preferred_element_type=jnp.float32
    )
    return product.astype(jnp.bfloat16)


def shards(
    table_cells,
    w_query,
    w_key,
    w_value,
    w_out,
    norm_gain,
    w_gate,
    w_up,
    w_down,
    lengths,
    expert_of_cell,
    slot_of_cell,
):
    cell_count, tables, model_width = table_cells.shape
    head_width = w_query.shape[1]
    head_count = head_width // DH
    score_scale = 1.0 / math.sqrt(DH)
    joined = jnp.concatenate([w_query, w_key, w_value], axis=1)
    shard_rows = lax.all_gather(table_cells, "head", axis=0, tiled=True)
    rows_here = shard_rows.shape[0]
    mixed_rows = jnp.dot(
        shard_rows.reshape(rows_here * tables, model_width),
        joined,
        preferred_element_type=jnp.float32,
    )
    projected = mixed_rows.astype(jnp.bfloat16).reshape(rows_here, tables, 3 * head_width)
    row_cells = projected.shape[0]
    queries = projected[:, :, :head_width].reshape(row_cells, tables, head_count, DH)
    key_rows = projected[:, :, head_width : 2 * head_width]
    value_rows = projected[:, :, 2 * head_width :]
    offset = lax.axis_index("expert") * row_cells
    own_positions = offset + jnp.arange(row_cells, dtype=jnp.int32)
    start_state = (
        jnp.full((tables, head_count, row_cells), -1e30, jnp.float32),
        jnp.zeros((tables, head_count, row_cells), jnp.float32),
        jnp.zeros((tables, head_count, row_cells, DH), jnp.float32),
    )
    key_piece = lax.all_gather(key_rows, "expert", axis=0, tiled=True)
    value_piece = lax.all_gather(value_rows, "expert", axis=0, tiled=True)
    piece_len = key_piece.shape[0]
    block_len = math.gcd(piece_len, 512)
    block_count = piece_len // block_len
    key_blocks = key_piece.reshape(block_count, block_len, tables, head_count, DH)
    value_blocks = value_piece.reshape(block_count, block_len, tables, head_count, DH)
    block_starts = jnp.arange(block_count, dtype=jnp.int32) * block_len

    def step(carried, block_item):
        running_max, running_sum, accum = carried
        key_block, value_block, block_first = block_item
        scores = (
            jnp.einsum("qshd,kshd->shqk", queries, key_block, preferred_element_type=jnp.float32)
            * score_scale
        )
        key_valid = (block_first + jnp.arange(block_len, dtype=jnp.int32))[None, :] < lengths[
            :, None
        ]
        scores = jnp.where(key_valid[:, None, None, :], scores, -jnp.inf)
        new_max = jnp.maximum(running_max, jnp.max(scores, axis=-1))
        factor = jnp.exp(running_max - new_max)
        exp_scores = jnp.exp(scores - new_max[..., None])
        running_sum = running_sum * factor + jnp.sum(exp_scores, axis=-1)
        accum = accum * factor[..., None] + jnp.einsum(
            "shqk,kshd->shqd",
            exp_scores.astype(jnp.bfloat16),
            value_block,
            preferred_element_type=jnp.float32,
        )
        return ((new_max, running_sum, accum), None)

    finished, _ = lax.scan(step, start_state, (key_blocks, value_blocks, block_starts))
    running_max, running_sum, accum = finished
    normalized = accum / running_sum[..., None]
    live = own_positions[None, :] < lengths[:, None]
    normalized = jnp.where(live[:, None, :, None], normalized, 0.0)
    attended = (
        jnp.transpose(normalized, (2, 0, 1, 3))
        .reshape(row_cells, tables, head_width)
        .astype(jnp.bfloat16)
    )
    count_rows = cell_count * lax.axis_size("head")
    product = jnp.dot(
        attended.reshape(count_rows * tables, head_width), w_out, preferred_element_type=jnp.float32
    )
    summed = lax.psum_scatter(
        product.reshape(count_rows, tables, model_width).astype(jnp.bfloat16),
        "head",
        scatter_dimension=0,
        tiled=True,
    ).astype(jnp.float32)
    residual = table_cells.astype(jnp.float32) + summed
    mean_square = jnp.mean(residual * residual, axis=-1, keepdims=True)
    normed = (residual * lax.rsqrt(mean_square + 1e-06) * norm_gain.astype(jnp.float32)).astype(
        jnp.bfloat16
    )
    rows_dev = cell_count * tables
    normed_rows = normed.reshape(rows_dev, model_width)
    expert_count = lax.axis_size("expert") * lax.axis_size("head") // 2
    slot_cap = 2 * max(1, rows_dev // expert_count)
    target = expert_of_cell.reshape(rows_dev) * slot_cap + slot_of_cell.reshape(rows_dev)
    slot_table = (
        jnp.arange(expert_count * slot_cap, dtype=jnp.int32)[:, None] == target[None, :]
    ).astype(jnp.bfloat16)
    send_rows = jnp.dot(slot_table, normed_rows, preferred_element_type=jnp.float32).astype(
        jnp.bfloat16
    )
    gate_half = w_gate[0]
    up_half = w_up[0]
    down_half = w_down[0]
    doubled = jnp.repeat(send_rows.reshape(expert_count, slot_cap, model_width), 2, axis=0)
    received = lax.all_to_all(doubled, ("expert", "head"), split_axis=0, concat_axis=0, tiled=True)
    sources = received.shape[0]
    item_count = received.shape[1]
    flat_rows = received.reshape(sources * item_count, model_width)
    gathered = lax.all_to_all(
        expert_half(flat_rows, gate_half, up_half, down_half).reshape(
            sources, item_count, model_width
        ),
        ("expert", "head"),
        split_axis=0,
        concat_axis=0,
        tiled=True,
    )
    halves = gathered.reshape(expert_count, 2, slot_cap, model_width).astype(jnp.float32)
    combined = (
        (halves[:, 0] + halves[:, 1])
        .astype(jnp.bfloat16)
        .reshape(expert_count * slot_cap, model_width)
    )
    expert_out = lax.dot_general(
        slot_table, combined, (((0,), (0,)), ((), ())), preferred_element_type=jnp.float32
    )
    updated = (residual.reshape(rows_dev, model_width) + expert_out).astype(jnp.bfloat16)
    return updated.reshape(cell_count, tables, model_width)


def solution(mesh):
    placed = (
        P(("expert", "head"), None, None),
        P(None, "head"),
        P(None, "head"),
        P(None, "head"),
        P("head", None),
        P(),
        P(("expert", "head"), None, None),
        P(("expert", "head"), None, None),
        P(("expert", "head"), None, None),
        P(),
        P(("expert", "head"), None),
        P(("expert", "head"), None),
    )
    return jax.shard_map(
        shards,
        mesh=mesh,
        in_specs=placed,
        out_specs=P(("expert", "head"), None, None),
        check_vma=False,
    )
```

profile of v0, /device:TPU:1, one launch (start us, length us, event | category | flops | bytes accessed | tf_op | source)
XLA Modules:
  0.0 631.7 jit_solution(11269988385761301558)
XLA Ops:
  7.3 37.8 %all-gather.4.cloned.1.call-done = bf16[512,2,2048]{2,1,0:T(2,128)(2,1)} async-done(((bf16[64,2,2048]{2,1,0:T(2,128)(2,1)}), bf16[512,2,2048]{2,1,0:T(2,128)(2,1)}) %all-gather.4.cloned.1.call-update) | async-done | bytes 4194320 | tf_op jit(solution)/shard_map/all_gather | solution.py:42
  45.1 7.2 %reshape.135 = bf16[1024,2048]{1,0:T(8,128)(2,1)} reshape(bf16[512,2,2048]{2,1,0:T(2,128)(2,1)} %all-gather.4.cloned.1.call-done) | data formatting | bytes 8388608 | tf_op jit(solution)/shard_map/reshape | solution.py:45
  52.3 7.8 %fusion.33 = bf16[1024,768]{0,1:T(8,128)(2,1)} fusion(bf16[1024,2048]{1,0:T(8,128)(2,1)} %reshape.135, bf16[2048,256]{1,0:T(8,128)(2,1)} %param.17, bf16[2048,256]{1,0:T(8,128)(2,1)} %param.16, bf16[2048,256]{1,0:T(8,128)(2,1)} %param.15), kind=kOutput, calls=%fused_computation.46 | convolution fusion | flops 3231449088 | bytes 8912896 | tf_op jit(solution)/shard_map/dot_general | solution.py:44
  62.7 4.5 reshape.136
  67.2 3.4 fusion.56
  74.5 66.3 %all-gather.6.cloned.1.call-done = bf16[8192,2,256]{2,1,0:T(2,128)(2,1)} async-done(((bf16[512,2,256]{2,1,0:T(2,128)(2,1)}), bf16[8192,2,256]{2,1,0:T(2,128)(2,1)}) %all-gather.6.cloned.1.call-update) | async-done | bytes 8388624 | tf_op jit(solution)/shard_map/all_gather | solution.py:61
  140.8 21.6 %reshape.149 = bf16[16,512,2,2,128]{4,3,2,1,0:T(2,128)(2,1)} reshape(bf16[8192,2,256]{2,1,0:T(2,128)(2,1)} %all-gather.6.cloned.1.call-done) | data formatting | bytes 16777216 | tf_op jit(solution)/shard_map/reshape | solution.py:66
  162.5 50.9 %all-gather.8.cloned.1.call-done = bf16[8192,2,256]{2,1,0:T(2,128)(2,1)} async-done(((bf16[512,2,256]{2,1,0:T(2,128)(2,1)}), bf16[8192,2,256]{2,1,0:T(2,128)(2,1)}) %all-gather.8.cloned.1.call-update) | async-done | bytes 8388624 | tf_op jit(solution)/shard_map/all_gather | solution.py:62
  213.3 21.6 %reshape.150 = bf16[16,512,2,2,128]{4,3,2,1,0:T(2,128)(2,1)} reshape(bf16[8192,2,256]{2,1,0:T(2,128)(2,1)} %all-gather.8.cloned.1.call-done) | data formatting | bytes 16777216 | tf_op jit(solution)/shard_map/reshape | solution.py:67
  234.9 227.6 %while.15 = (s32[]{:T(128)}, f32[2,2,512]{2,1,0:T(2,128)S(1)}, f32[2,2,512]{2,1,0:T(2,128)S(1)}, f32[2,2,512,128]{3,2,1,0:T(8,128)}, s32[16]{0:T(128)S(1)}, /*in...) while((s32[]{:T(128)}, f32[2,2,512]{2,1,0:T(2,128)S(1)}, ...), condition=%wide.region_3.4_spmd.clone, body=%wide.region_0.3_spmd.clone.sunk | while | flops 549203456 | bytes 35266736 | solution.py:93
  236.2 2.7 constant_dynamic-slice_fusion.3
  241.6 3.3 fusion.73
  245.1 3.8 fusion.75
  250.1 2.7 constant_dynamic-slice_fusion.3
  255.5 3.3 fusion.73
  259.0 4.1 fusion.75
  264.4 2.7 constant_dynamic-slice_fusion.3
  269.8 3.3 fusion.73
  273.2 4.1 fusion.75
  278.6 2.7 constant_dynamic-slice_fusion.3
  284.0 3.3 fusion.73
  287.5 4.1 fusion.75
  292.9 2.7 constant_dynamic-slice_fusion.3
  298.3 3.3 fusion.73
  301.7 4.1 fusion.75
  307.1 2.7 constant_dynamic-slice_fusion.3
  312.5 3.3 fusion.73
  316.0 4.1 fusion.75
  321.4 2.7 constant_dynamic-slice_fusion.3
  326.8 3.3 fusion.73
  330.2 4.1 fusion.75
  341.0 3.3 fusion.73
  344.5 4.1 fusion.75
  349.9 2.7 constant_dynamic-slice_fusion.3
  355.3 3.3 fusion.73
  358.7 4.1 fusion.75
  369.5 3.3 fusion.73
  373.0 4.1 fusion.75
  383.8 3.3 fusion.73
  387.2 4.1 fusion.75
  398.0 3.3 fusion.73
  401.5 4.1 fusion.75
  406.9 2.7 constant_dynamic-slice_fusion.3
  412.3 3.3 fusion.73
  415.7 4.1 fusion.75
  421.1 2.7 constant_dynamic-slice_fusion.3
  426.5 3.3 fusion.73
  430.0 4.1 fusion.75
  440.8 3.3 fusion.73
  444.2 4.1 fusion.75
  449.6 2.7 constant_dynamic-slice_fusion.3
  455.0 3.3 fusion.73
  458.5 4.1 fusion.75
  466.5 4.5 convolution_convert_fusion
  471.9 34.2 %reduce-scatter.2.cloned.1.call-done = bf16[64,2,2048]{2,0,1:T(8,128)(2,1)} async-done(((bf16[512,2,2048]{2,0,1:T(8,128)(2,1)}), bf16[64,2,2048]{2,0,1:T(8,128)(2,1)}) %reduce-scatter.2.cloned.1.call-update) | async-done | bytes 524304 | tf_op jit(solution)/shard_map/reduce_scatter | solution.py:107
  518.5 40.4 %all_to_all.10 = bf16[128,4,2048]{2,1,0:T(4,128)(2,1)} all-to-all(bf16[128,4,2048]{2,1,0:T(4,128)(2,1)S(1)} %bitcast.83), channel_id=1, replica_groups=mesh['expert'=16,'head'=8] {'expert','head'}, dimensions={0} | all-to-all | bytes 4194304 | tf_op jit(solution)/shard_map/all_to_all | solution.py:133
  558.9 4.0 reshape.144
  562.9 5.3 fusion.36
  568.1 7.6 %convolution_convert_fusion.1 = bf16[512,2048]{1,0:T(8,128)(2,1)} fusion(bf16[1,704,2048]{2,1,0:T(8,128)(2,1)S(1)} %copy-done, bf16[512,2048]{1,0:T(8,128)(2,1)} %reshape.144, bf16[1,704,2048]{2,1,0:T(8,128)(2,1)} %param.21, f32[704,512]{1,0:T(8,128)} %fusion.36), kind=kOutput, calls=%fused_computation.34 | convolution fusion | flops 2956001280 | bytes 11403264 | tf_op jit(solution)/shard_map/dot_general | solution.py:17
  575.8 4.1 reshape.145
  579.9 5.7 all-to-all-start.1
  585.5 3.0 copy.41
  588.5 2.9 reshape.140
  591.5 24.4 %all-to-all-done.1 = bf16[128,4,2048]{2,1,0:T(4,128)(2,1)} async-done(((bf16[128,4,2048]{2,1,0:T(4,128)(2,1)}), bf16[128,4,2048]{2,1,0:T(4,128)(2,1)}, u32[]{:S(2)}, u32[]{:S(2)}) %all-to-all-start.1) | async-done | bytes 2097184 | tf_op jit(solution)/shard_map/all_to_all | solution.py:137
  (197 shorter events, 113.7 us)
Async XLA Ops:
  6.5 561.6 %copy-start = (bf16[1,704,2048]{2,1,0:T(8,128)(2,1)S(1)}, bf16[1,704,2048]{2,1,0:T(8,128)(2,1)}, u32[]{:S(2)}) copy-start(bf16[1,704,2048]{2,1,0:T(8,128)(2,1)} %param.22) | copy-start | bytes 8650756
  6.5 38.5 %all-gather.4.cloned.1.call-start = ((), (), s32[]{:S(2)}) async-start(), calls=%async_computation.3 | async-start | bytes 4718592 | tf_op jit(solution)/shard_map/all_gather | solution.py:42
  7.3 133.5 %all-gather.6.cloned.1.call-start = ((), (), s32[]{:S(2)}) async-start(), calls=%async_computation.4 | async-start | bytes 8912896 | tf_op jit(solution)/shard_map/all_gather | solution.py:61
  62.7 9.0 %copy-start.3 = (s32[2]{0:T(128)S(1)}, s32[2]{0:T(128)}, u32[]{:S(2)}) copy-start(s32[2]{0:T(128)} %param.23) | copy-start | bytes 28
  70.7 142.7 %all-gather.8.cloned.1.call-start = ((), (), s32[]{:S(2)}) async-start(), calls=%async_computation.5 | async-start | bytes 8912896 | tf_op jit(solution)/shard_map/all_gather | solution.py:62
  71.4 434.7 %reduce-scatter.2.cloned.1.call-start = ((), (), s32[]{:S(2)}) async-start(), calls=%async_computation.6 | async-start | bytes 4718592 | tf_op jit(solution)/shard_map/reduce_scatter | solution.py:107
  241.6 3.4 copy-start.1
  255.5 3.4 copy-start.1
  269.8 3.4 copy-start.1
  284.0 3.4 copy-start.1
  298.3 3.4 copy-start.1
  312.5 3.4 copy-start.1
  326.8 3.4 copy-start.1
  341.0 3.4 copy-start.1
  355.3 3.4 copy-start.1
  369.5 3.4 copy-start.1
  383.8 3.4 copy-start.1
  398.0 3.4 copy-start.1
  412.3 3.4 copy-start.1
  426.5 3.4 copy-start.1
  440.8 3.4 copy-start.1
  455.0 3.4 copy-start.1
  471.0 0.7 copy-start.4
  471.0 0.7 copy-start.5
  471.0 0.7 copy-start.6
  471.0 35.2 %copy-start.2 = (bf16[64,2,2048]{2,1,0:T(2,128)(2,1)S(1)}, bf16[64,2,2048]{2,1,0:T(2,128)(2,1)}, u32[]{:S(2)}) copy-start(bf16[64,2,2048]{2,1,0:T(2,128)(2,1)} %param.14) | copy-start | bytes 1572868
  579.9 36.0 %all-to-all-start.1 = ((bf16[128,4,2048]{2,1,0:T(4,128)(2,1)}), bf16[128,4,2048]{2,1,0:T(4,128)(2,1)}, u32[]{:S(2)}, u32[]{:S(2)}) async-start(bf16[128,4,2048]{2,1,0:T(4,128)(2,1)} %reshape.145), calls=%async_computation.2 | async-start | bytes 4194304 | tf_op jit(solution)/shard_map/all_to_all | solution.py:137
Sparse Core Ops, SparseCore 0:
  9.1 35.9 all-gather.3
  70.8 69.9 all-gather.5
  143.0 70.3 all-gather.7
  471.1 34.9 reduce-scatter.1
where the time goes:
time: 635 us; the launch traced here: 632 us
  waiting for transfers between devices  215 us (34%)
  local copies, waits for them, and re-layouts  146 us (23%)
  matrix products  138 us (22%)
  other arithmetic  73.5 us (12%)
  blocking collectives  40.4 us (6%)
  between operations  13.2 us (2%)
    all_gather x1, waiting for transfers between devices, shards(): key_piece = lax.all_gather(key_rows, 'expert', axis=0, tiled=True)  66.3 us
    dot_general x16, matrix products, step(): jnp.einsum('shqk,kshd->shqd', exp_scores.astype(jnp.bfloat16), value_bloc...  65.2 us
    dynamic_slice x32, local copies, waits for them, and re-layouts, shards(): lax.scan(step, start_state, (key_blocks, value_blocks, block_starts))  52.7 us
    reduce_sum x16, other arithmetic, step(): running_sum = running_sum * factor + jnp.sum(exp_scores, axis=-1)  52.1 us
    all_gather x1, waiting for transfers between devices, shards(): value_piece = lax.all_gather(value_rows, 'expert', axis=0, tiled=True)  50.9 us
    dot_general x16, matrix products, step(): jnp.einsum('qshd,kshd->shqk', queries, key_block, preferred_element_type=...  42.8 us
    all_to_all x1, blocking collectives, shards(): lax.all_to_all(doubled, ('expert', 'head'), split_axis=0, concat_axis=0,...  40.4 us
    all_gather x1, waiting for transfers between devices, shards(): shard_rows = lax.all_gather(table_cells, 'head', axis=0, tiled=True)  37.8 us
  transfers between devices with their start and end apart: 5, of which 5 were waited for; matrix products, arithmetic and copies ran while one was open for 5% of the time, Pallas kernels for 0%

commit v1 on v0

--- a/solution.py
+++ b/solution.py
@@ -39,7 +39,25 @@
     head_count = head_width // DH
     score_scale = 1.0 / math.sqrt(DH)
     joined = jnp.concatenate([w_query, w_key, w_value], axis=1)
-    shard_rows = lax.all_gather(table_cells, "head", axis=0, tiled=True)
+    size, index, rows = (lax.axis_size("head"), lax.axis_index("head"), table_cells.shape[0])
+    forward = [(i, (i + 1) % size) for i in range(size)]
+    backward = [(i, (i - 1) % size) for i in range(size)]
+    shard_rows = jnp.zeros(
+        (*table_cells.shape[:0], size * rows, *table_cells.shape[0 + 1 :]), table_cells.dtype
+    )
+    shard_rows = lax.dynamic_update_slice_in_dim(shard_rows, table_cells, index * rows, axis=0)
+    from_left = from_right = table_cells
+    half = size // 2
+    for k in range(1, half + 1):
+        from_left = lax.ppermute(from_left, "head", forward)
+        shard_rows = lax.dynamic_update_slice_in_dim(
+            shard_rows, from_left, (index - k) % size * rows, axis=0
+        )
+        if k < size - half:
+            from_right = lax.ppermute(from_right, "head", backward)
+            shard_rows = lax.dynamic_update_slice_in_dim(
+                shard_rows, from_right, (index + k) % size * rows, axis=0
+            )
     rows_here = shard_rows.shape[0]
     mixed_rows = jnp.dot(
         shard_rows.reshape(rows_here * tables, model_width),

time: 635 us -> 638 us (level); the launches traced: 632 us -> 626 us
  local copies, waits for them, and re-layouts: 146 us -> 129 us
  waiting for transfers between devices: 215 us -> 199 us
  matrix products: 138 us -> 153 us
  starting transfers between devices: 5.97 us -> 16.6 us
    unnamed x13 -> x22, local copies, waits for them, and re-layouts: 2 us -> 58.1 us
    dynamic_slice x32 -> x16, local copies, waits for them, and re-layouts: 52.7 us -> 9.32 us  [shards(): lax.scan(step, start_state, (key_blocks, value_blocks, block_starts))]
    reshape x2 -> x0, local copies, waits for them, and re-layouts: 43.3 us -> none  [the longest x1 21.6 us: shards(): key_piece.reshape(block_count, block_len, tables, head_count, DH)]
    all_gather x1 -> x0, waiting for transfers between devices: 37.8 us -> none  [shards(): shard_rows = lax.all_gather(table_cells, 'head', axis=0, tiled=True)]
    dot_general x16, matrix products: 42.8 us -> 59.3 us  [step(): jnp.einsum('qshd,kshd->shqk', queries, key_block, preferred_element_type=...]
    dynamic_update_slice x0 -> x8, local copies, waits for them, and re-layouts: none -> 13.5 us  [the longest x4 6.74 us: shards(): lax.dynamic_update_slice_in_dim(shard_rows, from_left, (index - k) % size...]
    ppermute x0 -> x7, starting transfers between devices: none -> 10.4 us  [the longest x4 8.66 us: shards(): from_left = lax.ppermute(from_left, 'head', forward)]
    all_gather x1, waiting for transfers between devices: 66.3 us -> 76.6 us  [shards(): key_piece = lax.all_gather(key_rows, 'expert', axis=0, tiled=True)]
  transfers between devices with their start and end apart: 5 -> 11, of which waited for: 5 -> 8; matrix products, arithmetic and copies ran while one was open for 5% -> 8% of each run, Pallas kernels for 0% -> 0%
where the time goes in v1:
time: 638 us; the launch traced here: 626 us
  waiting for transfers between devices  199 us (31%)
  matrix products  153 us (24%)
  local copies, waits for them, and re-layouts  129 us (20%)
  other arithmetic  73.5 us (12%)
  blocking collectives  40.5 us (6%)
  starting transfers between devices  16.6 us (3%)
  between operations  13.5 us (2%)
    all_gather x1, waiting for transfers between devices, shards(): key_piece = lax.all_gather(key_rows, 'expert', axis=0, tiled=True)  76.6 us
    dot_general x16, matrix products, step(): jnp.einsum('shqk,kshd->shqd', exp_scores.astype(jnp.bfloat16), value_bloc...  64.6 us
    dot_general x16, matrix products, step(): jnp.einsum('qshd,kshd->shqk', queries, key_block, preferred_element_type=...  59.3 us
    unnamed x22, local copies, waits for them, and re-layouts  58.1 us
    all_gather x1, waiting for transfers between devices, shards(): value_piece = lax.all_gather(value_rows, 'expert', axis=0, tiled=True)  54.1 us
    reduce_sum x16, other arithmetic, step(): running_sum = running_sum * factor + jnp.sum(exp_scores, axis=-1)  52.1 us
    all_to_all x1, blocking collectives, shards(): lax.all_to_all(doubled, ('expert', 'head'), split_axis=0, concat_axis=0,...  40.5 us
    reduce_scatter x1, waiting for transfers between devices, shards(): lax.psum_scatter(product.reshape(count_rows, tables, model_width).astype(...  35.4 us
  transfers between devices with their start and end apart: 11, of which 8 were waited for; matrix products, arithmetic and copies ran while one was open for 8% of the time, Pallas kernels for 0%

profile of v1, /device:TPU:1, one launch (start us, length us, event | category | flops | bytes accessed | tf_op | source)
XLA Modules:
  0.0 626.4 jit_solution(13407108045165710774)
XLA Ops:
  9.6 6.4 %collective-permute-done = bf16[64,2,2048]{2,1,0:T(2,128)(2,1)} collective-permute-done((bf16[64,2,2048]{2,1,0:T(2,128)(2,1)}, bf16[64,2,2048]{2,1,0:T(2,128)(2,1)}, u32[]{:S(2)}, u32[]{:S(2)}) %collective-permute-start) | collective-permute-done | bytes 524320 | tf_op jit(solution)/shard_map/ppermute | solution.py:52
  18.7 4.1 broadcast_in_dim.54
  43.5 7.2 %reshape.135 = bf16[1024,2048]{1,0:T(8,128)(2,1)} reshape(bf16[512,2,2048]{2,1,0:T(2,128)(2,1)} %constant_dynamic-update-slice_fusion) | data formatting | bytes 8388608 | tf_op jit(solution)/shard_map/reshape | solution.py:63
  50.7 7.7 %fusion.36 = bf16[1024,768]{1,0:T(8,128)(2,1)} fusion(bf16[1024,2048]{1,0:T(8,128)(2,1)} %reshape.135, bf16[2048,256]{1,0:T(8,128)(2,1)} %param.17, bf16[2048,256]{1,0:T(8,128)(2,1)} %param.16, bf16[2048,256]{1,0:T(8,128)(2,1)} %param.15), kind=kOutput, calls=%fused_computation.47 | convolution fusion | flops 3231449088 | bytes 8912896 | tf_op jit(solution)/shard_map/dot_general | solution.py:62
  58.4 4.5 reshape.136
  63.0 3.4 fusion.59
  73.9 76.6 %all-gather.3.cloned.1.call-done = bf16[8192,2,256]{0,2,1:T(8,128)(2,1)} async-done(((bf16[512,2,256]{0,2,1:T(8,128)(2,1)}), bf16[8192,2,256]{0,2,1:T(8,128)(2,1)}) %all-gather.3.cloned.1.call-update) | async-done | bytes 8388624 | tf_op jit(solution)/shard_map/all_gather | solution.py:79
  150.5 11.0 %copy.34 = bf16[64,8,16,512]{3,2,1,0:T(8,128)(2,1)} copy(bf16[64,8,16,512]{3,1,2,0:T(8,128)(2,1)} %bitcast.95) | data formatting | bytes 16777216
  161.5 14.7 %copy.21 = bf16[16,512,2,2,128]{4,1,3,2,0:T(8,128)(2,1)} copy(bf16[16,512,2,2,128]{1,0,4,3,2:T(8,128)(2,1)} %bitcast.93) | data formatting | bytes 16777216
  176.2 54.1 %all-gather.5.cloned.1.call-done = bf16[8192,2,256]{0,2,1:T(8,128)(2,1)} async-done(((bf16[512,2,256]{0,2,1:T(8,128)(2,1)}), bf16[8192,2,256]{0,2,1:T(8,128)(2,1)}) %all-gather.5.cloned.1.call-update) | async-done | bytes 8388624 | tf_op jit(solution)/shard_map/all_gather | solution.py:80
  230.3 11.0 %copy.35 = bf16[64,8,16,512]{3,2,1,0:T(8,128)(2,1)} copy(bf16[64,8,16,512]{3,1,2,0:T(8,128)(2,1)} %bitcast.96) | data formatting | bytes 16777216
  241.3 14.6 %copy.23 = bf16[16,512,2,2,128]{4,1,3,2,0:T(8,128)(2,1)} copy(bf16[16,512,2,2,128]{1,0,4,3,2:T(8,128)(2,1)} %bitcast.94) | data formatting | bytes 16777216
  255.9 200.3 %while.15 = (s32[]{:T(128)}, f32[2,2,512]{2,1,0:T(2,128)S(1)}, f32[2,2,512]{2,1,0:T(2,128)S(1)}, f32[2,2,512,128]{3,2,1,0:T(8,128)}, s32[16]{0:T(128)S(1)}, /*in...) while((s32[]{:T(128)}, f32[2,2,512]{2,1,0:T(2,128)S(1)}, ...), condition=%wide.region_3.4_spmd.clone, body=%wide.region_0.3_spmd.clone.sunk | while | flops 549203456 | bytes 33170604 | solution.py:111
  257.4 3.7 bitcast_reduce_fusion.2
  261.1 3.3 fusion.78
  264.5 3.7 fusion.80
  269.6 3.7 bitcast_reduce_fusion.2
  273.3 3.3 fusion.78
  276.7 4.1 fusion.80
  282.1 3.7 bitcast_reduce_fusion.2
  285.8 3.3 fusion.78
  289.3 4.1 fusion.80
  294.6 3.7 bitcast_reduce_fusion.2
  298.4 3.3 fusion.78
  301.8 4.1 fusion.80
  307.2 3.7 bitcast_reduce_fusion.2
  310.9 3.3 fusion.78
  314.3 4.1 fusion.80
  319.7 3.7 bitcast_reduce_fusion.2
  323.4 3.3 fusion.78
  326.8 4.1 fusion.80
  332.2 3.7 bitcast_reduce_fusion.2
  335.9 3.3 fusion.78
  339.4 4.1 fusion.80
  344.7 3.7 bitcast_reduce_fusion.2
  351.9 4.1 fusion.80
  357.3 3.7 bitcast_reduce_fusion.2
  364.4 4.1 fusion.80
  369.8 3.7 bitcast_reduce_fusion.2
  377.0 4.1 fusion.80
  382.3 3.7 bitcast_reduce_fusion.2
  389.5 4.1 fusion.80
  394.9 3.7 bitcast_reduce_fusion.2
  402.0 4.1 fusion.80
  407.4 3.7 bitcast_reduce_fusion.2
  414.5 4.1 fusion.80
  419.9 3.7 bitcast_reduce_fusion.2
  423.6 3.3 fusion.78
  427.1 4.1 fusion.80
  432.4 3.7 bitcast_reduce_fusion.2
  436.2 3.3 fusion.78
  439.6 4.1 fusion.80
  445.0 3.7 bitcast_reduce_fusion.2
  448.7 3.3 fusion.78
  452.1 4.1 fusion.80
  460.1 4.5 convolution_convert_fusion
  465.0 35.4 %reduce-scatter.2.cloned.1.call-done = bf16[64,2,2048]{2,0,1:T(8,128)(2,1)} async-done(((bf16[512,2,2048]{2,0,1:T(8,128)(2,1)}), bf16[64,2,2048]{2,0,1:T(8,128)(2,1)}) %reduce-scatter.2.cloned.1.call-update) | async-done | bytes 524304 | tf_op jit(solution)/shard_map/reduce_scatter | solution.py:125
  512.8 40.5 %all_to_all.10 = bf16[128,4,2048]{2,1,0:T(4,128)(2,1)} all-to-all(bf16[128,4,2048]{2,1,0:T(4,128)(2,1)S(1)} %bitcast.97), channel_id=1, replica_groups=mesh['expert'=16,'head'=8] {'expert','head'}, dimensions={0} | all-to-all | bytes 4194304 | tf_op jit(solution)/shard_map/all_to_all | solution.py:151
  553.4 4.0 reshape.144
  557.4 5.3 fusion.39
  562.6 7.6 %convolution_convert_fusion.1 = bf16[512,2048]{1,0:T(8,128)(2,1)} fusion(bf16[1,704,2048]{2,1,0:T(8,128)(2,1)S(1)} %copy-done, bf16[512,2048]{1,0:T(8,128)(2,1)} %reshape.144, bf16[1,704,2048]{2,1,0:T(8,128)(2,1)} %param.21, f32[704,512]{1,0:T(8,128)} %fusion.39), kind=kOutput, calls=%fused_computation.36 | convolution fusion | flops 2956001280 | bytes 11403264 | tf_op jit(solution)/shard_map/dot_general | solution.py:17
  570.3 4.1 reshape.145
  574.4 5.7 all-to-all-start.1
  586.0 24.4 %all-to-all-done.1 = bf16[128,4,2048]{2,1,0:T(4,128)(2,1)} async-done(((bf16[128,4,2048]{2,1,0:T(4,128)(2,1)}), bf16[128,4,2048]{2,1,0:T(4,128)(2,1)}, u32[]{:S(2)}, u32[]{:S(2)}) %all-to-all-start.1) | async-done | bytes 2097184 | tf_op jit(solution)/shard_map/all_to_all | solution.py:155
  (206 shorter events, 108.9 us)
Async XLA Ops:
  6.5 556.1 %copy-start = (bf16[1,704,2048]{2,1,0:T(8,128)(2,1)S(1)}, bf16[1,704,2048]{2,1,0:T(8,128)(2,1)}, u32[]{:S(2)}) copy-start(bf16[1,704,2048]{2,1,0:T(8,128)(2,1)} %param.22) | copy-start | bytes 8650756
  6.5 16.3 %copy-start.2 = (bf16[64,2,2048]{2,1,0:T(2,128)(2,1)S(1)}, bf16[64,2,2048]{2,1,0:T(2,128)(2,1)}, u32[]{:S(2)}) copy-start(bf16[64,2,2048]{2,1,0:T(2,128)(2,1)} %param.14) | copy-start | bytes 1572868
  6.5 144.0 %all-gather.3.cloned.1.call-start = ((), (), s32[]{:S(2)}) async-start(), calls=%async_computation.3 | async-start | bytes 8912896 | tf_op jit(solution)/shard_map/all_gather | solution.py:79
  6.5 9.5 %collective-permute-start = (bf16[64,2,2048]{2,1,0:T(2,128)(2,1)}, bf16[64,2,2048]{2,1,0:T(2,128)(2,1)}, u32[]{:S(2)}, u32[]{:S(2)}) collective-permute-start(bf16[64,2,2048]{2,1,0:T(2,128)(2,1)} %param.14), channel_id=1, source_target_pairs={{0,1},{1,2},{2,3},{3,4},{4,5},{5,6},{6,7},{7,0},{8,9},{9,10},{10,1... | collective-permute-start | bytes 1572872 | tf_op jit(solution)/shard_map/ppermute | solution.py:52
  9.6 8.9 %collective-permute-start.1 = (bf16[64,2,2048]{2,1,0:T(2,128)(2,1)}, bf16[64,2,2048]{2,1,0:T(2,128)(2,1)}, u32[]{:S(2)}, u32[]{:S(2)}) collective-permute-start(bf16[64,2,2048]{2,1,0:T(2,128)(2,1)} %param.14), channel_id=1, source_target_pairs={{0,7},{1,0},{2,1},{3,2},{4,3},{5,4},{6,5},{7,6},{8,15},{9,8},{10,9... | collective-permute-start | bytes 1572872 | tf_op jit(solution)/shard_map/ppermute | solution.py:57
  16.0 8.9 %collective-permute-start.2 = (bf16[64,2,2048]{2,1,0:T(2,128)(2,1)}, bf16[64,2,2048]{2,1,0:T(2,128)(2,1)}, u32[]{:S(2)}, u32[]{:S(2)}) collective-permute-start(bf16[64,2,2048]{2,1,0:T(2,128)(2,1)} %collective-permute-done), channel_id=1, source_target_pairs={{0,1},{1,2},{2,3},{3,4},{4,5},{5,6},{6,7},{7,0},{8,9},{9,10},{10,1... | collective-permute-start | bytes 1572872 | tf_op jit(solution)/shard_map/ppermute | solution.py:52
  18.5 13.4 %collective-permute-start.3 = (bf16[64,2,2048]{2,1,0:T(2,128)(2,1)}, bf16[64,2,2048]{2,1,0:T(2,128)(2,1)}, u32[]{:S(2)}, u32[]{:S(2)}) collective-permute-start(bf16[64,2,2048]{2,1,0:T(2,128)(2,1)} %collective-permute-done.1), channel_id=1, source_target_pairs={{0,7},{1,0},{2,1},{3,2},{4,3},{5,4},{6,5},{7,6},{8,15},{9,8},{10,9... | collective-permute-start | bytes 1572872 | tf_op jit(solution)/shard_map/ppermute | solution.py:57
  24.9 10.6 %collective-permute-start.4 = (bf16[64,2,2048]{2,1,0:T(2,128)(2,1)}, bf16[64,2,2048]{2,1,0:T(2,128)(2,1)S(1)}, u32[]{:S(2)}, u32[]{:S(2)}) collective-permute-start(bf16[64,2,2048]{2,1,0:T(2,128)(2,1)} %collective-permute-done.2), channel_id=1, source_target_pairs={{0,1},{1,2},{2,3},{3,4},{4,5},{5,6},{6,7},{7,0},{8,9},{9,10},{10,1... | collective-permute-start | bytes 1572872 | tf_op jit(solution)/shard_map/ppermute | solution.py:52
  31.8 8.8 %collective-permute-start.5 = (bf16[64,2,2048]{2,1,0:T(2,128)(2,1)}, bf16[64,2,2048]{2,1,0:T(2,128)(2,1)S(1)}, u32[]{:S(2)}, u32[]{:S(2)}) collective-permute-start(bf16[64,2,2048]{2,1,0:T(2,128)(2,1)} %collective-permute-done.3), channel_id=1, source_target_pairs={{0,7},{1,0},{2,1},{3,2},{4,3},{5,4},{6,5},{7,6},{8,15},{9,8},{10,9... | collective-permute-start | bytes 1572872 | tf_op jit(solution)/shard_map/ppermute | solution.py:57
  35.6 6.8 %collective-permute-start.6 = (bf16[64,2,2048]{2,1,0:T(2,128)(2,1)S(1)}, bf16[64,2,2048]{2,1,0:T(2,128)(2,1)S(1)}, u32[]{:S(2)}, u32[]{:S(2)}) collective-permute-start(bf16[64,2,2048]{2,1,0:T(2,128)(2,1)S(1)} %collective-permute-done.4), channel_id=1, source_target_pairs={{0,1},{1,2},{2,3},{3,4},{4,5},{5,6},{6,7},{7,0},{8,9},{9,10},{10,1... | collective-permute-start | bytes 1572872 | tf_op jit(solution)/shard_map/ppermute | solution.py:52
  58.4 12.6 %copy-start.4 = (s32[2]{0:T(128)S(1)}, s32[2]{0:T(128)}, u32[]{:S(2)}) copy-start(s32[2]{0:T(128)} %param.23) | copy-start | bytes 28
  68.4 161.9 %all-gather.5.cloned.1.call-start = ((), (), s32[]{:S(2)}) async-start(), calls=%async_computation.4 | async-start | bytes 8912896 | tf_op jit(solution)/shard_map/all_gather | solution.py:80
  70.5 429.9 %reduce-scatter.2.cloned.1.call-start = ((), (), s32[]{:S(2)}) async-start(), calls=%async_computation.5 | async-start | bytes 4718592 | tf_op jit(solution)/shard_map/reduce_scatter | solution.py:125
  261.1 3.4 copy-start.1
  273.3 3.4 copy-start.1
  285.8 3.4 copy-start.1
  298.3 3.4 copy-start.1
  310.9 3.4 copy-start.1
  323.4 3.4 copy-start.1
  335.9 3.4 copy-start.1
  348.5 3.4 copy-start.1
  361.0 3.4 copy-start.1
  373.5 3.4 copy-start.1
  386.0 3.4 copy-start.1
  398.6 3.4 copy-start.1
  411.1 3.4 copy-start.1
  423.6 3.4 copy-start.1
  436.2 3.4 copy-start.1
  448.7 3.4 copy-start.1
  460.1 4.6 copy-start.5
  460.1 4.6 copy-start.6
  460.1 4.6 copy-start.7
  460.1 40.3 %copy-start.3 = (bf16[64,2,2048]{2,1,0:T(2,128)(2,1)S(1)}, bf16[64,2,2048]{2,1,0:T(2,128)(2,1)}, u32[]{:S(2)}) copy-start(bf16[64,2,2048]{2,1,0:T(2,128)(2,1)} %param.14) | copy-start | bytes 1572868
  574.4 36.0 %all-to-all-start.1 = ((bf16[128,4,2048]{2,1,0:T(4,128)(2,1)}), bf16[128,4,2048]{2,1,0:T(4,128)(2,1)}, u32[]{:S(2)}, u32[]{:S(2)}) async-start(bf16[128,4,2048]{2,1,0:T(4,128)(2,1)} %reshape.145), calls=%async_computation.2 | async-start | bytes 4194304 | tf_op jit(solution)/shard_map/all_to_all | solution.py:155
Sparse Core Ops, SparseCore 0:
  68.5 81.9 all-gather.2
  152.6 77.6 all-gather.4
  464.8 35.5 reduce-scatter.1
